TPU v7x, 128 devices: a whole 4x4x4 slice. The times are simulated.
128 devices in a mesh: src: 4 (over x_lo, core), tgt: 32 (over y, x_hi, z).
Axes of the slice: x: 4 (x_hi: 2, x_lo: 2; x = x_hi * 2 + x_lo), y: 4, z: 4, core: 2. Of those that a mesh axis runs over, the one named last changes fastest.
Arguments:
- source_feat: bfloat16 [16384, 256], P(('src', 'tgt')), may hold values from -40 to 40
- target_feat: bfloat16 [57600, 256], P('tgt', 'src'), may hold values from -4 to 4
- proj: bfloat16 [256, 256], replicated, may hold values from -0.375 to 0.375
Outputs:
- flow: float32 [2, 16384], P(None, ('src', 'tgt'))
- matched: bfloat16 [16384, 256], P(('src', 'tgt'))
All inputs are finite; a program needn't handle non-finite values.
Results may differ from a plain program's by a relative error of at most 0.0075.
Values may be sent and summed in bfloat16 or wider, within the bound.
A program may use at most 256 MiB of HBM per device.

v0:
```python
import jax
import jax.numpy as jnp
from jax import lax
from jax.sharding import PartitionSpec as P

W_GRID = 320


def grid_coords(pos):
    return (
        (pos % W_GRID).astype(jnp.float32) / W_GRID,
        (pos // W_GRID).astype(jnp.float32) / W_GRID,
    )


def partial_block(queries, keys, key_start):
    width = queries.shape[1]
    scores = jnp.einsum("qc,kc->qk", queries, keys, preferred_element_type=jnp.float32) * width ** (
        -0.5
    )
    top = jnp.max(scores, axis=1)
    weights = jnp.exp(scores - top[:, None])
    total = jnp.sum(weights, axis=1)
    pos = key_start + jnp.arange(keys.shape[0], dtype=jnp.int32)
    grid_x, grid_y = grid_coords(pos)
    coord_sum = jnp.stack(
        [jnp.sum(weights * grid_x[None, :], axis=1), jnp.sum(weights * grid_y[None, :], axis=1)],
        axis=0,
    )
    feat_sum = jnp.dot(weights.astype(jnp.bfloat16), keys, preferred_element_type=jnp.float32)
    return (top, total, coord_sum, feat_sum)


def per_device(source_feat, target_feat, proj):
    width = proj.shape[1]
    own_rows = source_feat.shape[0]
    tgt_rows = target_feat.shape[0]
    strips = lax.axis_size("tgt")
    queries = jnp.dot(source_feat, proj, preferred_element_type=jnp.float32).astype(jnp.bfloat16)
    keys = jnp.dot(
        lax.all_gather(target_feat, "src", axis=1, tiled=True),
        proj,
        preferred_element_type=jnp.float32,
    ).astype(jnp.bfloat16)
    own_start = (lax.axis_index("src") * strips + lax.axis_index("tgt")) * own_rows
    strip = lax.all_gather(queries, "tgt", axis=0, tiled=True)
    strip_rows = strip.shape[0]
    block = min(256, strip_rows)
    key_start = lax.axis_index("tgt") * tgt_rows

    def one_block(qblock):
        return partial_block(qblock, keys, key_start)

    top, total, coord_sum, feat_sum = lax.map(
        one_block, strip.reshape(strip_rows // block, block, width)
    )
    top = top.reshape(strip_rows)
    total = total.reshape(strip_rows)
    coord_sum = jnp.moveaxis(coord_sum, 1, 0).reshape(2, strip_rows)
    feat_sum = feat_sum.reshape(strip_rows, width)
    largest = lax.pmax(top, "tgt")
    rescale = jnp.exp(top - largest)
    total, coord_sum, feat_sum = (
        lax.psum_scatter(total * rescale, "tgt", scatter_dimension=0, tiled=True),
        lax.psum_scatter(coord_sum * rescale[None, :], "tgt", scatter_dimension=1, tiled=True),
        lax.psum_scatter(feat_sum * rescale[:, None], "tgt", scatter_dimension=0, tiled=True),
    )
    own_pos = own_start + jnp.arange(own_rows, dtype=jnp.int32)
    own_x, own_y = grid_coords(own_pos)
    flow = jnp.stack([coord_sum[0] / total - own_x, coord_sum[1] / total - own_y], axis=0)
    matched = (feat_sum / total[:, None]).astype(jnp.bfloat16)
    return (flow, matched)


def solution(mesh):
    in_specs = (P(("src", "tgt"), None), P("tgt", "src"), P())
    out_specs = (P(None, ("src", "tgt")), P(("src", "tgt"), None))
    return jax.shard_map(
        per_device, mesh=mesh, in_specs=in_specs, out_specs=out_specs, check_vma=False
    )
```

profile of v0, /device:TPU:0, one launch (start us, length us, event | category | flops | bytes accessed | tf_op | source)
XLA Modules:
  0.0 709.4 jit_solution(2130675689377072865)
XLA Ops:
  8.1 1.6 convolution_convert_fusion.1
  9.8 10.0 %all_gather.7 = bf16[1800,256]{0,1:T(8,128)(2,1)S(1)} all-gather(bf16[1800,64]{0,1:T(8,128)(2,1)} %param.6), channel_id=1, replica_groups=mesh['src'=4,'tgt'=32] {'src'}, dimensions={1}, use_global_device_ids=true | all-gather | bytes 1152000 | tf_op jit(solution)/shard_map/all_gather | solution.py:41
  20.2 64.7 %all-gather.2.cloned.1.call-done = bf16[4096,256]{1,0:T(8,128)(2,1)} async-done(((bf16[128,256]{1,0:T(8,128)(2,1)}), bf16[4096,256]{1,0:T(8,128)(2,1)}) %all-gather.2.cloned.1.call-update) | async-done | bytes 2097168 | tf_op jit(solution)/shard_map/all_gather | solution.py:46
  84.9 61.6 %while.18 = (s32[]{:T(128)}, f32[16,256]{1,0:T(8,128)S(1)}, f32[16,256]{1,0:T(8,128)S(1)}, f32[16,2,256]{2,1,0:T(2,128)S(1)}, f32[16,256,256]{2,1,0:T(8,128)}, /...) while((s32[]{:T(128)}, f32[16,256]{1,0:T(8,128)S(1)}, ...), condition=%wide.region_5.6_spmd, body=%wide.region_0.5_spmd.sunk | while | flops 476497280 | bytes 7810293 | solution.py:54
  84.9 1.4 fusion.44
  88.7 1.4 fusion.44
  92.6 1.4 fusion.44
  96.4 1.4 fusion.44
  99.0 1.3 fusion.47
  100.3 1.4 fusion.44
  104.1 1.4 fusion.44
  106.7 1.3 fusion.47
  108.0 1.4 fusion.44
  111.9 1.4 fusion.44
  114.4 1.3 fusion.47
  115.7 1.4 fusion.44
  119.6 1.4 fusion.44
  123.4 1.4 fusion.44
  126.0 1.3 fusion.47
  127.3 1.4 fusion.44
  129.8 1.3 fusion.47
  131.1 1.4 fusion.44
  135.0 1.4 fusion.44
  138.8 1.4 fusion.44
  142.7 1.4 fusion.44
  145.2 1.3 fusion.47
  146.5 180.2 %pmax.7 = f32[4096]{0:T(1024)S(1)} all-reduce(f32[4096]{0:T(1024)S(1)} %bitcast.74), channel_id=1, replica_groups=mesh['src'=4,'tgt'=32] {'tgt'}, use_global_device_ids=true, to_apply=%region_6.7 | all-reduce | flops 4096 | bytes 32768 | tf_op jit(solution)/shard_map/pmax | solution.py:61
  326.8 2.1 copy.5
  329.0 3.9 bitcast_multiply_fusion
  334.8 176.2 %all-reduce = f32[4096]{0:T(1024)S(1)} all-reduce(f32[4096]{0:T(1024)S(1)} %get-tuple-element.134), channel_id=3, replica_groups=mesh['src'=4,'tgt'=32] {'tgt'}, use_global_device_ids=true, to_apply=%region_8.9.clone | all-reduce | flops 4096 | bytes 32768
  513.2 188.0 %reduce-scatter.5.cloned.1.call-done = f32[128,256]{1,0:T(8,128)} async-done(((f32[4096,256]{1,0:T(8,128)}), f32[128,256]{1,0:T(8,128)}) %reduce-scatter.5.cloned.1.call-update) | async-done | bytes 131088 | tf_op jit(solution)/shard_map/reduce_scatter | solution.py:66
  701.2 1.6 divide_convert_fusion
  (117 shorter events, 35.7 us)
Async XLA Ops:
  7.2 0.9 copy-start
  7.2 77.7 %all-gather.2.cloned.1.call-start = ((), (), s32[]{:S(2)}) async-start(), calls=%async_computation.2 | async-start | bytes 2162688 | tf_op jit(solution)/shard_map/all_gather | solution.py:46
  9.7 501.6 %reduce-scatter.7.cloned.1.call-start = ((), (), s32[]{:S(2)}) async-start(), calls=%async_computation.4 | async-start | bytes 2162688
  328.9 372.3 %reduce-scatter.5.cloned.1.call-start = ((), (), s32[]{:S(2)}) async-start(), calls=%async_computation.3 | async-start | bytes 4325376 | tf_op jit(solution)/shard_map/reduce_scatter | solution.py:66
  332.9 0.7 copy-start.1
Sparse Core Ops, SparseCore 0:
  11.7 73.2 all-gather.1
  329.0 182.2 reduce-scatter.6
  513.9 187.2 reduce-scatter.4
where the time goes:
time: 710 us; the launch traced here: 709 us
  blocking collectives  366 us (52%)
  waiting for transfers between devices  253 us (36%)
  matrix products  44.9 us (6%)
  other arithmetic  23.4 us (3%)
  between operations  14.5 us (2%)
    reduce_scatter x1, waiting for transfers between devices, per_device(): lax.psum_scatter(feat_sum * rescale[:, None], 'tgt', scatter_dimension=0,...  188 us
    pmax x1, blocking collectives, per_device(): largest = lax.pmax(top, 'tgt')  180 us
    unnamed x1, blocking collectives  176 us
    all_gather x1, waiting for transfers between devices, per_device(): strip = lax.all_gather(queries, 'tgt', axis=0, tiled=True)  64.7 us
    dot_general x16, matrix products, partial_block(): jnp.einsum('qc,kc->qk', queries, keys, preferred_element_type=jnp.float32)  22.6 us
    dot_general x16, matrix products, partial_block(): jnp.dot(weights.astype(jnp.bfloat16), keys, preferred_element_type=jnp.fl...  20.2 us
    reduce_sum x16, other arithmetic, partial_block(): jnp.sum(weights * grid_x[None, :], axis=1)  16.6 us
  transfers between devices with their start and end apart: 3, of which 3 were waited for; matrix products, arithmetic and copies ran while one was open for 1% of the time, Pallas kernels for 0%

commit v1 on v0

--- a/solution.py
+++ b/solution.py
@@ -43,7 +43,9 @@
         preferred_element_type=jnp.float32,
     ).astype(jnp.bfloat16)
     own_start = (lax.axis_index("src") * strips + lax.axis_index("tgt")) * own_rows
-    strip = lax.all_gather(queries, "tgt", axis=0, tiled=True)
+    strip = jnp.concatenate(
+        lax.all_to_all(jnp.stack([queries] * lax.axis_size("tgt")), "tgt", 0, 0), axis=0
+    )
     strip_rows = strip.shape[0]
     block = min(256, strip_rows)
     key_start = lax.axis_index("tgt") * tgt_rows

time: 710 us -> 679 us (0.956)
  waiting for transfers between devices: 253 us -> 187 us
  blocking collectives: 366 us -> 389 us
  starting transfers between devices: 0.12 us -> 11.2 us
    all_gather x1 -> x0, waiting for transfers between devices: 64.7 us -> none  [per_device(): strip = lax.all_gather(queries, 'tgt', axis=0, tiled=True)]
    all_gather x1, blocking collectives: 9.96 us -> 29.4 us  [per_device(): lax.all_gather(target_feat, 'src', axis=1, tiled=True)]
    all_to_all x0 -> x1, starting transfers between devices: none -> 11.1 us  [per_device(): lax.all_to_all(jnp.stack([queries] * lax.axis_size('tgt')), 'tgt', 0, 0)]
  transfers between devices with their start and end apart: 3 -> 3, of which waited for: 3 -> 2; matrix products, arithmetic and copies ran while one was open for 1% -> 1% of each run, Pallas kernels for 0% -> 0%
where the time goes in v1:
time: 679 us
  blocking collectives  389 us (57%)
  waiting for transfers between devices  187 us (28%)
  matrix products  44.3 us (7%)
  other arithmetic  23.4 us (3%)
  between operations  14.8 us (2%)
  starting transfers between devices  11.2 us (2%)
  local copies, waits for them, and re-layouts  7.93 us (1%)
    reduce_scatter x1, waiting for transfers between devices, per_device(): lax.psum_scatter(feat_sum * rescale[:, None], 'tgt', scatter_dimension=0,...  187 us
    pmax x1, blocking collectives, per_device(): largest = lax.pmax(top, 'tgt')  184 us
    unnamed x1, blocking collectives  176 us
    all_gather x1, blocking collectives, per_device(): lax.all_gather(target_feat, 'src', axis=1, tiled=True)  29.4 us
    dot_general x16, matrix products, partial_block(): jnp.einsum('qc,kc->qk', queries, keys, preferred_element_type=jnp.float32)  22.7 us
    dot_general x16, matrix products, partial_block(): jnp.dot(weights.astype(jnp.bfloat16), keys, preferred_element_type=jnp.fl...  20.2 us
    reduce_sum x16, other arithmetic, partial_block(): jnp.sum(weights * grid_x[None, :], axis=1)  16.6 us
  transfers between devices with their start and end apart: 3, of which 2 were waited for; matrix products, arithmetic and copies ran while one was open for 1% of the time, Pallas kernels for 0%

profile of v1, /device:TPU:0, one launch (start us, length us, event | category | flops | bytes accessed | tf_op | source)
XLA Modules:
  0.0 678.6 jit_solution(1946889032732983868)
XLA Ops:
  9.1 1.5 stack.23
  10.6 11.1 %all-to-all-start = ((bf16[32,128,256]{2,1,0:T(8,128)(2,1)}), bf16[32,128,256]{2,1,0:T(8,128)(2,1)}, u32[]{:S(2)}, u32[]{:S(2)}) async-start(bf16[32,128,256]{2,1,0:T(8,128)(2,1)} %stack.23), calls=%async_computation | async-start | bytes 4194304 | tf_op jit(solution)/shard_map/all_to_all | solution.py:47
  21.9 29.4 %all_gather.3 = bf16[1800,256]{0,1:T(8,128)(2,1)S(1)} all-gather(bf16[1800,64]{0,1:T(8,128)(2,1)S(1)} %copy-done.1), channel_id=1, replica_groups=mesh['src'=4,'tgt'=32] {'src'}, dimensions={1}, use_global_device_ids=true | all-gather | bytes 1152000 | tf_op jit(solution)/shard_map/all_gather | solution.py:41
  52.3 61.7 %while.18 = (s32[]{:T(128)}, f32[16,256]{1,0:T(8,128)S(1)}, f32[16,256]{1,0:T(8,128)S(1)}, f32[16,2,256]{2,1,0:T(2,128)S(1)}, f32[16,256,256]{2,1,0:T(8,128)}, /...) while((s32[]{:T(128)}, f32[16,256]{1,0:T(8,128)S(1)}, ...), condition=%wide.region_5.6_spmd, body=%wide.region_0.5_spmd.sunk | while | flops 476497280 | bytes 7810293 | solution.py:56
  52.3 1.4 fusion.44
  56.1 1.4 fusion.44
  60.0 1.4 fusion.44
  63.8 1.4 fusion.44
  66.4 1.3 fusion.47
  67.7 1.4 fusion.44
  71.5 1.4 fusion.44
  74.1 1.3 fusion.47
  75.4 1.4 fusion.44
  79.3 1.4 fusion.44
  81.8 1.3 fusion.47
  83.1 1.4 fusion.44
  87.0 1.4 fusion.44
  90.8 1.4 fusion.44
  93.4 1.3 fusion.47
  94.7 1.4 fusion.44
  97.2 1.3 fusion.47
  98.6 1.4 fusion.44
  102.4 1.4 fusion.44
  106.3 1.4 fusion.44
  110.1 1.4 fusion.44
  112.7 1.3 fusion.47
  114.0 183.6 %pmax.7 = f32[4096]{0:T(1024)S(1)} all-reduce(f32[4096]{0:T(1024)S(1)} %bitcast.73), channel_id=1, replica_groups=mesh['src'=4,'tgt'=32] {'tgt'}, use_global_device_ids=true, to_apply=%region_6.7 | all-reduce | flops 4096 | bytes 32768 | tf_op jit(solution)/shard_map/pmax | solution.py:63
  297.7 2.1 copy.5
  299.8 3.9 bitcast_multiply_fusion
  305.6 176.2 %all-reduce = f32[4096]{0:T(1024)S(1)} all-reduce(f32[4096]{0:T(1024)S(1)} %get-tuple-element.134), channel_id=3, replica_groups=mesh['src'=4,'tgt'=32] {'tgt'}, use_global_device_ids=true, to_apply=%region_8.9.clone | all-reduce | flops 4096 | bytes 32768
  483.6 186.6 %reduce-scatter.5.cloned.1.call-done = f32[128,256]{1,0:T(8,128)} async-done(((f32[4096,256]{1,0:T(8,128)}), f32[128,256]{1,0:T(8,128)}) %reduce-scatter.5.cloned.1.call-update) | async-done | bytes 131088 | tf_op jit(solution)/shard_map/reduce_scatter | solution.py:68
  670.2 1.6 divide_convert_fusion
  (119 shorter events, 37.0 us)
Async XLA Ops:
  7.2 0.9 copy-start
  10.6 11.2 %copy-start.1 = (bf16[1800,64]{0,1:T(8,128)(2,1)S(1)}, bf16[1800,64]{0,1:T(8,128)(2,1)}, u32[]{:S(2)}) copy-start(bf16[1800,64]{0,1:T(8,128)(2,1)} %param.6) | copy-start | bytes 691204
  10.6 41.7 %all-to-all-start = ((bf16[32,128,256]{2,1,0:T(8,128)(2,1)}), bf16[32,128,256]{2,1,0:T(8,128)(2,1)}, u32[]{:S(2)}, u32[]{:S(2)}) async-start(bf16[32,128,256]{2,1,0:T(8,128)(2,1)} %stack.23), calls=%async_computation | async-start | bytes 4194304 | tf_op jit(solution)/shard_map/all_to_all | solution.py:47
  21.8 460.0 %reduce-scatter.7.cloned.1.call-start = ((), (), s32[]{:S(2)}) async-start(), calls=%async_computation.4 | async-start | bytes 2162688
  299.8 370.4 %reduce-scatter.5.cloned.1.call-start = ((), (), s32[]{:S(2)}) async-start(), calls=%async_computation.3 | async-start | bytes 4325376 | tf_op jit(solution)/shard_map/reduce_scatter | solution.py:68
  303.7 0.7 copy-start.2
Sparse Core Ops, SparseCore 0:
  299.9 180.7 reduce-scatter.6
  483.2 186.9 reduce-scatter.4
